TPU v7x, 128 devices: a whole 4x4x4 slice. The times are simulated.
128 devices in a mesh: space: 32 (over y, x, core), tx: 4 (over z).
Axes of the slice: x: 4, y: 4, z: 4, core: 2. Of those that a mesh axis runs over, the one named last changes fastest.
Arguments:
- conductivity: float32 [64, 128, 256], P('space'), may hold values from 0.25 to 2
- chargeability: float32 [64, 128, 256], P('space'), may hold values from 0.05 to 0.6
- relaxation: float32 [64, 128, 256], P('space'), may hold values from 0.5 to 8
- start_potential: float32 [8, 64, 128, 256], P('tx', 'space'), may hold values from 0 to 2
- start_memory: float32 [4, 8, 64, 128, 256], P(None, 'tx', 'space'), may hold values from -6 to 6
- source_cells: int32 [2, 8], P(None, 'tx'), may hold values from 0 to 2097151
- dipole_cells: int32 [2, 4096], replicated, may hold values from 0 to 2097151
- live_counts: int32 [32], replicated, may hold values from 32 to 128, as said below
- observed: float32 [3, 8, 4096], P(None, 'tx', 'space'), may hold values from -4 to 4
Outputs:
- voltages: float32 [3, 8, 4096], P(None, 'tx', 'space')
- misfit: float32 [], replicated
- grad_chargeability: float32 [64, 128, 256], P('space', 'tx')
- grad_relaxation: float32 [64, 128, 256], P('space', 'tx')
Inputs may be any that keep to these rules, and one draw needn't show every extreme that they name: `source_cells`: flat cell indices of the grid. `dipole_cells`: flat cell indices of the grid. `live_counts`: some slab has all 128 slots live.
All inputs are finite; a program needn't handle non-finite values.
Results may differ from a plain program's by a relative error of at most 0.00002.
Values sent between devices are 32-bit elements; how exact they have to be, the bound alone decides.
A program may use at most 192 MiB of HBM per device.

v0:
```python
import jax
import jax.numpy as jnp
from jax import lax
from jax.sharding import PartitionSpec as P

NSTEPS = 3
JACOBI = 8
mode_weights = (0.4, 0.3, 0.2, 0.1)
mode_ratios = (0.25, 1.0, 4.0, 16.0)
strength = 4.0


def extended(array, sides, width):
    for axis, dim in sides:
        peers, length = (lax.axis_size(axis), array.shape[dim])
        up = [(i, (i + 1) % peers) for i in range(peers - 1)]
        down = [(j, i) for i, j in up]
        last = lax.slice_in_dim(array, length - width, length, axis=dim)
        initial = lax.slice_in_dim(array, 0, width, axis=dim)
        before = lax.ppermute(last, axis, up)
        after = lax.ppermute(initial, axis, down)
        array = jnp.concatenate([before, array, after], axis=dim)
    return array


def neighbours(padded):
    core = padded[:, 1:-1]
    total = padded[:, 2:] + padded[:, :-2]
    side_y = jnp.pad(core, ((0, 0), (0, 0), (1, 1), (0, 0)))
    total = total + side_y[:, :, 2:] + side_y[:, :, :-2]
    side_z = jnp.pad(core, ((0, 0), (0, 0), (0, 0), (1, 1)))
    return total + side_z[..., 2:] + side_z[..., :-2]


def rim_one(field):
    return extended(field, (("space", 1),), 1)


def total_misfit(partial_value):
    return jnp.sqrt(1.0 + lax.psum(partial_value, ("space", "tx")))


def on_device(
    conductivity,
    chargeability,
    relaxation,
    start_potential,
    start_memory,
    source_cells,
    dipole_cells,
    live_counts,
    observed,
):
    slots = start_potential.shape[0]
    cells = conductivity.size
    tile = lax.axis_index("space")
    first = tile * cells
    inverse = 1.0 / (6.0 + conductivity)

    def local_index(global_cells):
        shifted = global_cells - first
        inside = ((shifted >= 0) & (shifted < cells)).astype(jnp.float32)
        return (jnp.clip(shifted, 0, cells - 1), inside)

    slot_ids = jnp.arange(slots, dtype=jnp.int32)
    place_a, inside_a = local_index(source_cells[0])
    place_b, inside_b = local_index(source_cells[1])
    source = jnp.zeros((slots, cells), jnp.float32).at[slot_ids, place_a].add(strength * inside_a)
    source = source.at[slot_ids, place_b].add(-strength * inside_b).reshape(start_potential.shape)
    probe_one, inside_one = local_index(dipole_cells[0])
    probe_two, inside_two = local_index(dipole_cells[1])
    decays = [jnp.exp(-1.0 / (relaxation * ratio)) for ratio in mode_ratios]
    couple = [chargeability * mode_weights[level] * (1.0 - decays[level]) for level in range(4)]
    slopes = [decays[level] / (mode_ratios[level] * relaxation * relaxation) for level in range(4)]
    memory = [start_memory[level] for level in range(4)]
    potential = start_potential
    kept_potential = []
    kept_memory = []
    partials = []
    for step in range(NSTEPS):
        stored = memory[0] + memory[1] + memory[2] + memory[3]
        if step == 0:
            rhs = source + conductivity * stored
        else:
            rhs = conductivity * stored
        forward_field = potential
        for forward_sweep in range(JACOBI):
            forward_field = (rhs + neighbours(rim_one(forward_field))) * inverse
        potential = forward_field
        kept_potential.append(potential)
        kept_memory.append(memory)
        memory = [decays[level] * memory[level] + couple[level] * potential for level in range(4)]
        flat = potential.reshape(slots, cells)
        partials.append(
            jnp.take(flat, probe_one, axis=1) * inside_one
            - jnp.take(flat, probe_two, axis=1) * inside_two
        )
    volts = lax.psum_scatter(jnp.stack(partials), "space", scatter_dimension=2, tiled=True)
    receivers = observed.shape[2]
    live = (jnp.arange(receivers) < live_counts[tile]).astype(jnp.float32)
    volts = volts * live
    resid = live * (volts - observed)
    partial_value = jnp.sum(resid * resid)
    misfit = total_misfit(partial_value)
    pulled = resid / misfit
    spread = lax.all_gather(pulled, "space", axis=2, tiled=True)
    back = jnp.zeros_like(start_potential)
    duals = [jnp.zeros_like(start_potential) for level in range(4)]
    grad_c = jnp.zeros_like(start_potential)
    grad_t = jnp.zeros_like(start_potential)
    for step in reversed(range(NSTEPS)):
        current = kept_potential[step]
        before = kept_memory[step]
        inject = jnp.zeros((slots, cells), jnp.float32)
        inject = inject.at[:, probe_one].add(spread[step] * inside_one)
        inject = (
            inject.at[:, probe_two].add(-spread[step] * inside_two).reshape(start_potential.shape)
        )
        incoming = back + inject
        for level in range(4):
            incoming = incoming + couple[level] * duals[level]
            grad_c = grad_c + duals[level] * mode_weights[level] * (1.0 - decays[level]) * current
            grad_t = grad_t + duals[level] * slopes[level] * (
                before[level] - chargeability * mode_weights[level] * current
            )
        duals = [decays[level] * duals[level] for level in range(4)]
        field = incoming
        summed = jnp.zeros_like(incoming)
        for sweep in range(JACOBI):
            scaled = field * inverse
            summed = summed + scaled
            field = neighbours(rim_one(scaled))
        summed, back = (summed, field)
        duals = [duals[level] + conductivity * summed for level in range(4)]
    grad_charge, grad_relax = (
        lax.psum_scatter(jnp.sum(grad_c, axis=0), "tx", scatter_dimension=1, tiled=True),
        lax.psum_scatter(jnp.sum(grad_t, axis=0), "tx", scatter_dimension=1, tiled=True),
    )
    return (volts, misfit, grad_charge, grad_relax)


def solution(mesh):
    placed = (
        P("space", None, None),
        P("space", None, None),
        P("space", None, None),
        P("tx", "space", None, None),
        P(None, "tx", "space", None, None),
        P(None, "tx"),
        P(),
        P(),
        P(None, "tx", "space"),
    )
    return jax.shard_map(
        on_device,
        mesh=mesh,
        in_specs=placed,
        out_specs=(P(None, "tx", "space"), P(), P("space", "tx", None), P("space", "tx", None)),
        check_vma=False,
    )
```

profile of v0, /device:TPU:0, one launch (start us, length us, event | category | flops | bytes accessed | tf_op | source)
XLA Modules:
  0.0 1156.9 jit_solution(7150294656307960920)
XLA Ops:
  171.0 9.5 collective-permute-start.33
  183.8 9.3 collective-permute-start.35
  195.9 9.3 collective-permute-start.37
  258.2 10.0 collective-permute-start.47
  268.2 16.6 %copy.44 = f32[2,2,128,256]{0,3,2,1:T(8,128)} copy(f32[2,2,128,256]{3,2,1,0:T(8,128)S(1)} %fusion.73) | data formatting | bytes 1048576 | tf_op jit(solution)/shard_map/mul | solution.py:88
  284.8 24.7 %gather_fusion.1 = f32[4096,2]{1,0:T(8,128)} fusion(f32[2,65536]{0,1:T(8,128)} %bitcast.195, s32[4096]{0:T(1024)S(1)} %fusion.321), kind=kCustom, calls=%fused_computation.1.clone | custom fusion | bytes 81920 | tf_op jit(solution)/shard_map/jit(_take)/gather | solution.py:96
  309.5 24.7 %gather_fusion = f32[4096,2]{1,0:T(8,128)} fusion(f32[2,65536]{0,1:T(8,128)} %bitcast.196, s32[4096]{0:T(1024)S(1)} %fusion.320), kind=kCustom, calls=%fused_computation.clone | custom fusion | bytes 81920 | tf_op jit(solution)/shard_map/jit(_take)/gather | solution.py:95
  334.2 17.4 %copy.45 = f32[2,2,128,256]{0,3,2,1:T(8,128)} copy(f32[2,2,128,256]{3,2,1,0:T(8,128)} %copy-done.1) | data formatting | bytes 1048576 | tf_op jit(solution)/shard_map/mul | solution.py:88
  351.6 24.7 %gather_fusion.3 = f32[4096,2]{1,0:T(8,128)} fusion(f32[2,65536]{0,1:T(8,128)} %bitcast.197, s32[4096]{0:T(1024)S(1)} %fusion.321), kind=kCustom, calls=%fused_computation.3.clone | custom fusion | bytes 81920 | tf_op jit(solution)/shard_map/jit(_take)/gather | solution.py:96
  376.4 24.7 %gather_fusion.2 = f32[4096,2]{1,0:T(8,128)} fusion(f32[2,65536]{0,1:T(8,128)} %bitcast.198, s32[4096]{0:T(1024)S(1)} %fusion.320), kind=kCustom, calls=%fused_computation.2.clone | custom fusion | bytes 81920 | tf_op jit(solution)/shard_map/jit(_take)/gather | solution.py:95
  404.7 17.4 %copy.46 = f32[2,2,128,256]{0,3,2,1:T(8,128)} copy(f32[2,2,128,256]{3,2,1,0:T(8,128)} %fusion.169) | data formatting | bytes 1048576 | tf_op jit(solution)/shard_map/mul | solution.py:88
  422.2 24.7 %gather_fusion.5 = f32[4096,2]{1,0:T(8,128)} fusion(f32[2,65536]{0,1:T(8,128)} %bitcast.193, s32[4096]{0:T(1024)S(1)} %fusion.321), kind=kCustom, calls=%fused_computation.5.clone | custom fusion | bytes 81920 | tf_op jit(solution)/shard_map/jit(_take)/gather | solution.py:96
  446.9 24.7 %gather_fusion.4 = f32[4096,2]{1,0:T(8,128)} fusion(f32[2,65536]{0,1:T(8,128)} %bitcast.194, s32[4096]{0:T(1024)S(1)} %fusion.320), kind=kCustom, calls=%fused_computation.4.clone | custom fusion | bytes 81920 | tf_op jit(solution)/shard_map/jit(_take)/gather | solution.py:95
  482.5 119.5 %reduce-scatter.4.cloned.1.call-done = f32[3,2,128]{1,2,0:T(8,128)} async-done(((f32[3,2,4096]{1,2,0:T(8,128)}), f32[3,2,128]{1,2,0:T(8,128)}) %reduce-scatter.4.cloned.1.call-update) | async-done | bytes 3088 | tf_op jit(solution)/shard_map/reduce_scatter | solution.py:98
  603.7 64.8 %psum.7 = f32[]{:T(128)} all-reduce(f32[]{:T(128)} %multiply_reduce_fusion), channel_id=1, replica_groups=mesh['space'=32,'tx'=4] {'space','tx'}, use_global_device_ids=true, to_apply=%region_4.6 | all-reduce | flops 1 | bytes 8 | tf_op jit(solution)/shard_map/psum | solution.py:40
  671.0 31.1 %all_gather.3 = f32[3,2,4096]{1,2,0:T(8,128)} all-gather(f32[3,2,128]{1,2,0:T(8,128)S(1)} %get-tuple-element.175), channel_id=1, replica_groups=mesh['space'=32,'tx'=4] {'space'}, dimensions={2}, use_global_device_ids=true | all-gather | bytes 101376 | tf_op jit(solution)/shard_map/all_gather | solution.py:106
  702.1 43.5 %scatter_custom_fusion.2 = f32[2,65536]{0,1:T(8,128)} fusion(s32[4096]{0:T(1024)S(1)} %bitcast.213, f32[]{:T(128)} %constant.26.clone.1, f32[3,2,4096]{1,2,0:T(8,128)} %all_gather.3, f32[4096]{0:T(1024)S(1)} %bitcast.205), kind=kCustom, calls=%fused_computation.14 | custom fusion | flops 16384 | bytes 2638336 | tf_op jit(solution)/shard_map/scatter-add | solution.py:115
  745.6 51.9 %scatter_custom_fusion.3 = f32[2,65536]{0,1:T(8,128)} fusion(f32[2,65536]{0,1:T(8,128)} %scatter_custom_fusion.2, s32[4096]{0:T(1024)S(1)} %bitcast.211, f32[3,2,4096]{1,2,0:T(8,128)} %all_gather.3, f32[4096]{0:T(1024)S(1)} %bitcast.202), kind=kCustom, calls=%fused_computation.22 | custom fusion | flops 24576 | bytes 2637824 | tf_op jit(solution)/shard_map/scatter-add | solution.py:117
  797.6 19.4 %copy.49 = f32[2,2,128,256]{3,2,1,0:T(8,128)S(1)} copy(f32[2,2,128,256]{0,3,2,1:T(8,128)} %bitcast.192) | data formatting | bytes 1048576 | tf_op jit(solution)/shard_map/reshape | solution.py:117
  892.3 43.7 %scatter_custom_fusion.4 = f32[2,65536]{0,1:T(8,128)} fusion(s32[4096]{0:T(1024)S(1)} %bitcast.214, f32[]{:T(128)} %constant.26.clone.1, f32[3,2,4096]{1,2,0:T(8,128)} %all_gather.3, f32[4096]{0:T(1024)S(1)} %bitcast.206), kind=kCustom, calls=%fused_computation.12 | custom fusion | flops 16384 | bytes 2638336 | tf_op jit(solution)/shard_map/scatter-add | solution.py:115
  935.9 51.9 %scatter_custom_fusion.5 = f32[2,65536]{0,1:T(8,128)} fusion(f32[2,65536]{0,1:T(8,128)} %scatter_custom_fusion.4, s32[4096]{0:T(1024)S(1)} %bitcast.212, f32[3,2,4096]{1,2,0:T(8,128)} %all_gather.3, f32[4096]{0:T(1024)S(1)} %bitcast.203), kind=kCustom, calls=%fused_computation.19 | custom fusion | flops 24576 | bytes 2637824 | tf_op jit(solution)/shard_map/scatter-add | solution.py:117
  987.9 20.2 %copy.51 = f32[2,2,128,256]{3,2,1,0:T(8,128)} copy(f32[2,2,128,256]{0,3,2,1:T(8,128)} %bitcast.191) | data formatting | bytes 1048576 | tf_op jit(solution)/shard_map/reshape | solution.py:117
  1091.9 33.7 %reduce-scatter.8.cloned.1.call-done = f32[2,32,256]{2,1,0:T(8,128)} async-done(((f32[2,128,256]{2,1,0:T(8,128)}), f32[2,32,256]{2,1,0:T(8,128)}) %reduce-scatter.8.cloned.1.call-update) | async-done | bytes 65552 | tf_op jit(solution)/shard_map/reduce_scatter | solution.py:137
  1125.6 23.5 %reduce-scatter.6.cloned.1.call-done = f32[2,32,256]{2,1,0:T(8,128)} async-done(((f32[2,128,256]{2,1,0:T(8,128)}), f32[2,32,256]{2,1,0:T(8,128)}) %reduce-scatter.6.cloned.1.call-update) | async-done | bytes 65552 | tf_op jit(solution)/shard_map/reduce_scatter | solution.py:136
  (379 shorter events, 397.7 us)
Async XLA Ops:
  7.2 594.9 %reduce-scatter.4.cloned.1.call-start = ((), (), s32[]{:S(2)}) async-start(), calls=%async_computation.3 | async-start | bytes 6488064 | tf_op jit(solution)/shard_map/reduce_scatter | solution.py:98
  86.8 11.5 collective-permute-start.16
  147.4 10.4 collective-permute-start.28
  148.7 10.2 collective-permute-start.29
  169.7 10.8 collective-permute-start.32
  171.0 10.4 collective-permute-start.33
  182.5 10.6 collective-permute-start.34
  183.8 10.4 collective-permute-start.35
  194.6 10.6 collective-permute-start.36
  195.9 10.4 collective-permute-start.37
  206.7 10.6 collective-permute-start.38
  208.0 10.4 collective-permute-start.39
  218.9 10.6 collective-permute-start.40
  220.2 10.4 collective-permute-start.41
  231.1 10.7 collective-permute-start.42
  232.4 10.4 collective-permute-start.43
  243.2 10.7 collective-permute-start.44
  244.5 10.4 collective-permute-start.45
  256.9 144.2 %collective-permute-start.46 = (f32[2,1,128,256]{3,2,1,0:T(8,128)}, f32[2,1,128,256]{3,2,1,0:T(8,128)}, u32[]{:S(2)}, u32[]{:S(2)}) collective-permute-start(f32[2,1,128,256]{3,2,1,0:T(8,128)} %get-tuple-element.81), channel_id=1, source_target_pairs={{4,0},{8,4},{12,8},{16,12},{20,16},{24,20},{28,24},{32,28},{36,32}... | collective-permute-start | bytes 786440 | tf_op jit(solution)/shard_map/ppermute | solution.py:21
  258.2 142.9 %collective-permute-start.47 = (f32[2,1,128,256]{3,2,1,0:T(8,128)}, f32[2,1,128,256]{3,2,1,0:T(8,128)}, u32[]{:S(2)}, u32[]{:S(2)}) collective-permute-start(f32[2,1,128,256]{3,2,1,0:T(8,128)} %get-tuple-element.82), channel_id=1, source_target_pairs={{0,4},{4,8},{8,12},{12,16},{16,20},{20,24},{24,28},{28,32},{32,36}... | collective-permute-start | bytes 786440 | tf_op jit(solution)/shard_map/ppermute | solution.py:20
  480.5 645.1 %reduce-scatter.8.cloned.1.call-start = ((), (), s32[]{:S(2)}) async-start(), calls=%async_computation.5 | async-start | bytes 327680 | tf_op jit(solution)/shard_map/reduce_scatter | solution.py:137
  883.1 125.0 %collective-permute-start.62 = (f32[2,1,128,256]{3,2,1,0:T(8,128)}, f32[2,1,128,256]{3,2,1,0:T(8,128)}, u32[]{:S(2)}, u32[]{:S(2)}) collective-permute-start(f32[2,1,128,256]{3,2,1,0:T(8,128)} %get-tuple-element.65), channel_id=1, source_target_pairs={{4,0},{8,4},{12,8},{16,12},{20,16},{24,20},{28,24},{32,28},{36,32}... | collective-permute-start | bytes 786440 | tf_op jit(solution)/shard_map/ppermute | solution.py:21
  884.4 123.7 %collective-permute-start.63 = (f32[2,1,128,256]{3,2,1,0:T(8,128)}, f32[2,1,128,256]{3,2,1,0:T(8,128)}, u32[]{:S(2)}, u32[]{:S(2)}) collective-permute-start(f32[2,1,128,256]{3,2,1,0:T(8,128)} %get-tuple-element.66), channel_id=1, source_target_pairs={{0,4},{4,8},{8,12},{12,16},{16,20},{20,24},{24,28},{28,32},{32,36}... | collective-permute-start | bytes 786440 | tf_op jit(solution)/shard_map/ppermute | solution.py:20
  1087.2 61.8 %reduce-scatter.6.cloned.1.call-start = ((), (), s32[]{:S(2)}) async-start(), calls=%async_computation.4 | async-start | bytes 327680 | tf_op jit(solution)/shard_map/reduce_scatter | solution.py:136
  (117 other events, 2069.6 us)
Sparse Core Ops, SparseCore 0:
  480.6 121.4 reduce-scatter.3
  1087.4 38.1 reduce-scatter.7
  1128.5 20.4 reduce-scatter.5
where the time goes:
time: 1170 us; the launch traced here: 1160 us
  starting transfers between devices  332 us (28%)
  other arithmetic  249 us (21%)
  local copies, waits for them, and re-layouts  248 us (21%)
  waiting for transfers between devices  215 us (18%)
  blocking collectives  96 us (8%)
  between operations  18 us (2%)
    ppermute x39, starting transfers between devices, extended(): before = lax.ppermute(last, axis, up)  280 us
    reduce_scatter x1, waiting for transfers between devices, on_device(): lax.psum_scatter(jnp.stack(partials), 'space', scatter_dimension=2, tiled...  120 us
    scatter-add x2, other arithmetic, on_device(): inject.at[:, probe_two].add(-spread[step] * inside_two)  104 us
    scatter-add x2, other arithmetic, on_device(): inject = inject.at[:, probe_one].add(spread[step] * inside_one)  87.2 us
    gather x3, local copies, waits for them, and re-layouts, on_device(): jnp.take(flat, probe_one, axis=1) * inside_one  74.2 us
    gather x3, local copies, waits for them, and re-layouts, on_device(): jnp.take(flat, probe_two, axis=1) * inside_two  74.1 us
    psum x1, blocking collectives, total_misfit(): return jnp.sqrt(1.0 + lax.psum(partial_value, ('space', 'tx')))  64.8 us
    mul x3, local copies, waits for them, and re-layouts, on_device(): forward_field = (rhs + neighbours(rim_one(forward_field))) * inverse  51.4 us
  transfers between devices with their start and end apart: 81, of which 38 were waited for; matrix products, arithmetic and copies ran while one was open for 23% of the time, Pallas kernels for 0%

commit v1 on v0

--- a/solution.py
+++ b/solution.py
@@ -37,7 +37,13 @@
 
 
 def total_misfit(partial_value):
-    return jnp.sqrt(1.0 + lax.psum(partial_value, ("space", "tx")))
+
+    def switch_sectors_over_axis(matrix):
+        for kk in ("space", "tx"):
+            matrix = lax.psum(matrix, kk)
+        return matrix
+
+    return jnp.sqrt(1.0 + switch_sectors_over_axis(partial_value))
 
 
 def on_device(

time: 1170 us -> 1180 us (level)
    psum x1 -> x2, blocking collectives: 64.8 us -> 75 us  [switch_sectors_over_axis(): matrix = lax.psum(matrix, kk)]
  transfers between devices with their start and end apart: 81 -> 81, of which waited for: 38 -> 38; matrix products, arithmetic and copies ran while one was open for 23% -> 22% of each run, Pallas kernels for 0% -> 0%
where the time goes in v1:
time: 1180 us; the launch traced here: 1170 us
  starting transfers between devices  332 us (28%)
  other arithmetic  249 us (21%)
  local copies, waits for them, and re-layouts  247 us (21%)
  waiting for transfers between devices  215 us (18%)
  blocking collectives  106 us (9%)
  between operations  18 us (2%)
    ppermute x39, starting transfers between devices, extended(): before = lax.ppermute(last, axis, up)  280 us
    reduce_scatter x1, waiting for transfers between devices, on_device(): lax.psum_scatter(jnp.stack(partials), 'space', scatter_dimension=2, tiled...  119 us
    scatter-add x2, other arithmetic, on_device(): inject.at[:, probe_two].add(-spread[step] * inside_two)  104 us
    scatter-add x2, other arithmetic, on_device(): inject = inject.at[:, probe_one].add(spread[step] * inside_one)  87.2 us
    psum x2, blocking collectives, switch_sectors_over_axis(): matrix = lax.psum(matrix, kk)  75 us
    gather x3, local copies, waits for them, and re-layouts, on_device(): jnp.take(flat, probe_two, axis=1) * inside_two  73.9 us
    gather x3, local copies, waits for them, and re-layouts, on_device(): jnp.take(flat, probe_one, axis=1) * inside_one  73.9 us
    mul x3, local copies, waits for them, and re-layouts, on_device(): forward_field = (rhs + neighbours(rim_one(forward_field))) * inverse  51.2 us
  transfers between devices with their start and end apart: 81, of which 38 were waited for; matrix products, arithmetic and copies ran while one was open for 22% of the time, Pallas kernels for 0%

profile of v1, /device:TPU:0, one launch (start us, length us, event | category | flops | bytes accessed | tf_op | source)
XLA Modules:
  0.0 1166.0 jit_solution(10166218158989652179)
XLA Ops:
  171.1 9.5 collective-permute-start.33
  183.8 9.3 collective-permute-start.35
  258.2 10.0 collective-permute-start.47
  268.2 16.5 %copy.44 = f32[2,2,128,256]{0,3,2,1:T(8,128)} copy(f32[2,2,128,256]{3,2,1,0:T(8,128)S(1)} %fusion.73) | data formatting | bytes 1048576 | tf_op jit(solution)/shard_map/mul | solution.py:94
  284.7 24.7 %gather_fusion.1 = f32[4096,2]{1,0:T(8,128)} fusion(f32[2,65536]{0,1:T(8,128)} %bitcast.195, s32[4096]{0:T(1024)S(1)} %fusion.321), kind=kCustom, calls=%fused_computation.1.clone | custom fusion | bytes 81920 | tf_op jit(solution)/shard_map/jit(_take)/gather | solution.py:102
  309.4 24.6 %gather_fusion = f32[4096,2]{1,0:T(8,128)} fusion(f32[2,65536]{0,1:T(8,128)} %bitcast.196, s32[4096]{0:T(1024)S(1)} %fusion.320), kind=kCustom, calls=%fused_computation.clone | custom fusion | bytes 81920 | tf_op jit(solution)/shard_map/jit(_take)/gather | solution.py:101
  334.1 17.3 %copy.45 = f32[2,2,128,256]{0,3,2,1:T(8,128)} copy(f32[2,2,128,256]{3,2,1,0:T(8,128)} %copy-done.1) | data formatting | bytes 1048576 | tf_op jit(solution)/shard_map/mul | solution.py:94
  351.4 24.6 %gather_fusion.3 = f32[4096,2]{1,0:T(8,128)} fusion(f32[2,65536]{0,1:T(8,128)} %bitcast.197, s32[4096]{0:T(1024)S(1)} %fusion.321), kind=kCustom, calls=%fused_computation.3.clone | custom fusion | bytes 81920 | tf_op jit(solution)/shard_map/jit(_take)/gather | solution.py:102
  376.0 24.6 %gather_fusion.2 = f32[4096,2]{1,0:T(8,128)} fusion(f32[2,65536]{0,1:T(8,128)} %bitcast.198, s32[4096]{0:T(1024)S(1)} %fusion.320), kind=kCustom, calls=%fused_computation.2.clone | custom fusion | bytes 81920 | tf_op jit(solution)/shard_map/jit(_take)/gather | solution.py:101
  404.1 17.3 %copy.46 = f32[2,2,128,256]{0,3,2,1:T(8,128)} copy(f32[2,2,128,256]{3,2,1,0:T(8,128)} %fusion.169) | data formatting | bytes 1048576 | tf_op jit(solution)/shard_map/mul | solution.py:94
  421.5 24.6 %gather_fusion.5 = f32[4096,2]{1,0:T(8,128)} fusion(f32[2,65536]{0,1:T(8,128)} %bitcast.193, s32[4096]{0:T(1024)S(1)} %fusion.321), kind=kCustom, calls=%fused_computation.5.clone | custom fusion | bytes 81920 | tf_op jit(solution)/shard_map/jit(_take)/gather | solution.py:102
  446.1 24.6 %gather_fusion.4 = f32[4096,2]{1,0:T(8,128)} fusion(f32[2,65536]{0,1:T(8,128)} %bitcast.194, s32[4096]{0:T(1024)S(1)} %fusion.320), kind=kCustom, calls=%fused_computation.4.clone | custom fusion | bytes 81920 | tf_op jit(solution)/shard_map/jit(_take)/gather | solution.py:101
  481.7 119.5 %reduce-scatter.4.cloned.1.call-done = f32[3,2,128]{1,2,0:T(8,128)} async-done(((f32[3,2,4096]{1,2,0:T(8,128)}), f32[3,2,128]{1,2,0:T(8,128)}) %reduce-scatter.4.cloned.1.call-update) | async-done | bytes 3088 | tf_op jit(solution)/shard_map/reduce_scatter | solution.py:104
  602.8 63.7 %psum.14 = f32[]{:T(128)} all-reduce(f32[]{:T(128)} %multiply_reduce_fusion), channel_id=1, replica_groups=mesh['space'=32,'tx'=4] {'space'}, use_global_device_ids=true, to_apply=%region_4.6 | all-reduce | flops 1 | bytes 8 | tf_op jit(solution)/shard_map/psum | solution.py:43
  666.5 11.3 psum.15
  680.2 31.2 %all_gather.3 = f32[3,2,4096]{1,2,0:T(8,128)} all-gather(f32[3,2,128]{1,2,0:T(8,128)S(1)} %get-tuple-element.175), channel_id=1, replica_groups=mesh['space'=32,'tx'=4] {'space'}, dimensions={2}, use_global_device_ids=true | all-gather | bytes 101376 | tf_op jit(solution)/shard_map/all_gather | solution.py:112
  711.4 43.5 %scatter_custom_fusion.2 = f32[2,65536]{0,1:T(8,128)} fusion(s32[4096]{0:T(1024)S(1)} %bitcast.213, f32[]{:T(128)} %constant.26.clone.1, f32[3,2,4096]{1,2,0:T(8,128)} %all_gather.3, f32[4096]{0:T(1024)S(1)} %bitcast.205), kind=kCustom, calls=%fused_computation.14 | custom fusion | flops 16384 | bytes 2638336 | tf_op jit(solution)/shard_map/scatter-add | solution.py:121
  755.0 51.9 %scatter_custom_fusion.3 = f32[2,65536]{0,1:T(8,128)} fusion(f32[2,65536]{0,1:T(8,128)} %scatter_custom_fusion.2, s32[4096]{0:T(1024)S(1)} %bitcast.211, f32[3,2,4096]{1,2,0:T(8,128)} %all_gather.3, f32[4096]{0:T(1024)S(1)} %bitcast.202), kind=kCustom, calls=%fused_computation.22 | custom fusion | flops 24576 | bytes 2637824 | tf_op jit(solution)/shard_map/scatter-add | solution.py:123
  806.9 19.4 %copy.49 = f32[2,2,128,256]{3,2,1,0:T(8,128)S(1)} copy(f32[2,2,128,256]{0,3,2,1:T(8,128)} %bitcast.192) | data formatting | bytes 1048576 | tf_op jit(solution)/shard_map/reshape | solution.py:123
  901.6 43.7 %scatter_custom_fusion.4 = f32[2,65536]{0,1:T(8,128)} fusion(s32[4096]{0:T(1024)S(1)} %bitcast.214, f32[]{:T(128)} %constant.26.clone.1, f32[3,2,4096]{1,2,0:T(8,128)} %all_gather.3, f32[4096]{0:T(1024)S(1)} %bitcast.206), kind=kCustom, calls=%fused_computation.12 | custom fusion | flops 16384 | bytes 2638336 | tf_op jit(solution)/shard_map/scatter-add | solution.py:121
  945.3 51.9 %scatter_custom_fusion.5 = f32[2,65536]{0,1:T(8,128)} fusion(f32[2,65536]{0,1:T(8,128)} %scatter_custom_fusion.4, s32[4096]{0:T(1024)S(1)} %bitcast.212, f32[3,2,4096]{1,2,0:T(8,128)} %all_gather.3, f32[4096]{0:T(1024)S(1)} %bitcast.203), kind=kCustom, calls=%fused_computation.19 | custom fusion | flops 24576 | bytes 2637824 | tf_op jit(solution)/shard_map/scatter-add | solution.py:123
  997.3 20.2 %copy.51 = f32[2,2,128,256]{3,2,1,0:T(8,128)} copy(f32[2,2,128,256]{0,3,2,1:T(8,128)} %bitcast.191) | data formatting | bytes 1048576 | tf_op jit(solution)/shard_map/reshape | solution.py:123
  1101.4 33.3 %reduce-scatter.8.cloned.1.call-done = f32[2,32,256]{2,1,0:T(8,128)} async-done(((f32[2,128,256]{2,1,0:T(8,128)}), f32[2,32,256]{2,1,0:T(8,128)}) %reduce-scatter.8.cloned.1.call-update) | async-done | bytes 65552 | tf_op jit(solution)/shard_map/reduce_scatter | solution.py:143
  1134.7 23.5 %reduce-scatter.6.cloned.1.call-done = f32[2,32,256]{2,1,0:T(8,128)} async-done(((f32[2,128,256]{2,1,0:T(8,128)}), f32[2,32,256]{2,1,0:T(8,128)}) %reduce-scatter.6.cloned.1.call-update) | async-done | bytes 65552 | tf_op jit(solution)/shard_map/reduce_scatter | solution.py:142
  (380 shorter events, 407.0 us)
Async XLA Ops:
  7.2 594.0 %reduce-scatter.4.cloned.1.call-start = ((), (), s32[]{:S(2)}) async-start(), calls=%async_computation.3 | async-start | bytes 6488064 | tf_op jit(solution)/shard_map/reduce_scatter | solution.py:104
  86.8 11.4 collective-permute-start.16
  147.4 10.3 collective-permute-start.28
  148.7 10.1 collective-permute-start.29
  169.8 10.8 collective-permute-start.32
  171.1 10.4 collective-permute-start.33
  182.5 10.6 collective-permute-start.34
  183.8 10.4 collective-permute-start.35
  194.6 10.6 collective-permute-start.36
  195.9 10.4 collective-permute-start.37
  206.8 10.6 collective-permute-start.38
  208.1 10.4 collective-permute-start.39
  218.9 10.6 collective-permute-start.40
  220.2 10.4 collective-permute-start.41
  231.1 10.7 collective-permute-start.42
  232.4 10.4 collective-permute-start.43
  243.2 10.7 collective-permute-start.44
  244.5 10.4 collective-permute-start.45
  256.9 143.7 %collective-permute-start.46 = (f32[2,1,128,256]{3,2,1,0:T(8,128)}, f32[2,1,128,256]{3,2,1,0:T(8,128)}, u32[]{:S(2)}, u32[]{:S(2)}) collective-permute-start(f32[2,1,128,256]{3,2,1,0:T(8,128)} %get-tuple-element.81), channel_id=1, source_target_pairs={{4,0},{8,4},{12,8},{16,12},{20,16},{24,20},{28,24},{32,28},{36,32}... | collective-permute-start | bytes 786440 | tf_op jit(solution)/shard_map/ppermute | solution.py:21
  258.2 142.5 %collective-permute-start.47 = (f32[2,1,128,256]{3,2,1,0:T(8,128)}, f32[2,1,128,256]{3,2,1,0:T(8,128)}, u32[]{:S(2)}, u32[]{:S(2)}) collective-permute-start(f32[2,1,128,256]{3,2,1,0:T(8,128)} %get-tuple-element.82), channel_id=1, source_target_pairs={{0,4},{4,8},{8,12},{12,16},{16,20},{20,24},{24,28},{28,32},{32,36}... | collective-permute-start | bytes 786440 | tf_op jit(solution)/shard_map/ppermute | solution.py:20
  479.6 655.1 %reduce-scatter.8.cloned.1.call-start = ((), (), s32[]{:S(2)}) async-start(), calls=%async_computation.5 | async-start | bytes 327680 | tf_op jit(solution)/shard_map/reduce_scatter | solution.py:143
  892.5 125.0 %collective-permute-start.62 = (f32[2,1,128,256]{3,2,1,0:T(8,128)}, f32[2,1,128,256]{3,2,1,0:T(8,128)}, u32[]{:S(2)}, u32[]{:S(2)}) collective-permute-start(f32[2,1,128,256]{3,2,1,0:T(8,128)} %get-tuple-element.65), channel_id=1, source_target_pairs={{4,0},{8,4},{12,8},{16,12},{20,16},{24,20},{28,24},{32,28},{36,32}... | collective-permute-start | bytes 786440 | tf_op jit(solution)/shard_map/ppermute | solution.py:21
  893.8 123.7 %collective-permute-start.63 = (f32[2,1,128,256]{3,2,1,0:T(8,128)}, f32[2,1,128,256]{3,2,1,0:T(8,128)}, u32[]{:S(2)}, u32[]{:S(2)}) collective-permute-start(f32[2,1,128,256]{3,2,1,0:T(8,128)} %get-tuple-element.66), channel_id=1, source_target_pairs={{0,4},{4,8},{8,12},{12,16},{16,20},{20,24},{24,28},{28,32},{32,36}... | collective-permute-start | bytes 786440 | tf_op jit(solution)/shard_map/ppermute | solution.py:20
  1096.7 61.4 %reduce-scatter.6.cloned.1.call-start = ((), (), s32[]{:S(2)}) async-start(), calls=%async_computation.4 | async-start | bytes 327680 | tf_op jit(solution)/shard_map/reduce_scatter | solution.py:142
  (117 other events, 2070.1 us)
Sparse Core Ops, SparseCore 0:
  479.7 121.3 reduce-scatter.3
  1096.8 37.7 reduce-scatter.7
  1137.6 20.4 reduce-scatter.5
